TPU v7x, 32 devices: a whole 2x2x4 slice. The times are simulated.
32 devices in a mesh: op: 4 (over y, x), str: 8 (over z, core).
Axes of the slice: x: 2, y: 2, z: 4, core: 2. Of those that a mesh axis runs over, the one named last changes fastest.
Arguments:
- coeffs: float32 [4096, 4096], P('str'), may hold values from -6 to 6
- previous: float32 [4096, 4096], P('str'), may hold values from -6 to 6
- block_values: bfloat16 [4, 32, 6, 128, 128], P('op'), may hold values from -0.21875 to 0.21875
- block_cols: int32 [4, 32, 6], P('op'), may hold values from 0 to 31, as said below
Outputs:
- advanced: float32 [4096, 4096], P('str')
Inputs may be any that keep to these rules, and one draw needn't show every extreme that they name: For every term k and block row r, block_cols[k, r, 0] equals r and the 6 entries of block_cols[k, r] are distinct.
All inputs are finite; a program needn't handle non-finite values.
Results may differ from a plain program's by a relative error of at most 0.0003.
Values sent between devices are 32-bit elements; how exact they have to be, the bound alone decides.
A program may use at most 192 MiB of HBM per device.

v0:
```python
import math
import jax
import jax.numpy as jnp
from jax import lax
from jax.sharding import PartitionSpec as P

STEPS = 2


def per_device(coeffs, previous, block_values, block_cols):
    local_terms = block_values.shape[0]
    step_scale = 2.0 / math.sqrt(local_terms * lax.axis_size("op"))
    factors = block_values.astype(jnp.float32)
    row_count, full_width = coeffs.shape
    block_size = block_values.shape[-1]
    block_count = full_width // block_size
    slot_count = block_cols.shape[2]
    regrouped = lax.all_to_all(
        previous.reshape(row_count, block_count, block_size),
        "str",
        split_axis=1,
        concat_axis=0,
        tiled=True,
    )
    earlier = regrouped.reshape(full_width, row_count).T
    current = coeffs
    for step_index in range(STEPS):
        column_list = block_cols[0].reshape(-1)
        term_factors = factors[0]
        gathered = jnp.take(
            current.reshape(row_count, block_count, block_size), column_list, axis=1
        )
        gathered = gathered.reshape(row_count, block_count, slot_count, block_size)
        beta_side = jnp.einsum(
            "arjc,rjoc->aro", gathered, term_factors, precision=lax.Precision.HIGHEST
        )
        received = lax.all_to_all(beta_side, "str", split_axis=1, concat_axis=0, tiled=True)
        group_count = received.shape[1]
        item_count = received.shape[2]
        grouped = jnp.take(
            received.reshape(block_count, block_size, group_count, item_count), column_list, axis=0
        )
        grouped = grouped.reshape(block_count, slot_count, block_size, group_count, item_count)
        result = jnp.einsum(
            "rjoc,rjcnm->nmro", term_factors, grouped, precision=lax.Precision.HIGHEST
        )
        moved = result.reshape(group_count, item_count, full_width)
        summed = moved.reshape(row_count, full_width)
        updated = step_scale * lax.psum(summed, "op") - earlier
        earlier, current = (current, updated)
    return current


def solution(mesh):
    placed = (P("str", None), P("str", None), P("op", None, None, None, None), P("op", None, None))
    return jax.shard_map(
        per_device, mesh=mesh, in_specs=placed, out_specs=P("str", None), check_vma=False
    )
```

profile of v0, /device:TPU:0, one launch (start us, length us, event | category | flops | bytes accessed | tf_op | source)
XLA Modules:
  0.0 1236.2 jit_solution(6269851794979325475)
XLA Ops:
  7.4 9.0 copy.26
  16.4 9.0 copy.27
  25.3 22.2 %gather_fusion = f32[192,512,128]{2,1,0:T(8,128)} fusion(f32[512,32,128]{2,0,1:T(8,128)} %copy.27, s32[1024]{0:T(1024)S(1)} %pad_clamp_fusion), kind=kCustom, calls=%fused_computation.clone | custom fusion | bytes 100664064 | tf_op jit(solution)/shard_map/jit(_take)/gather | solution.py:30
  47.6 34.0 %broadcast_select_fusion.3 = f32[192,512,128]{2,1,0:T(8,128)} fusion(f32[192,512,128]{2,1,0:T(8,128)} %gather_fusion, pred[192]{0:T(512)(128)(4,1)S(1)} %compare_and_fusion), kind=kLoop, calls=%fused_computation.7 | loop fusion | flops 12582912 | bytes 100663488 | tf_op jit(solution)/shard_map/jit(_take)/select_n | solution.py:30
  81.6 30.1 %fusion.8 = f32[512,32,128]{2,0,1:T(8,128)} fusion(f32[512,32,6,128]{3,0,2,1:T(8,128)} %bitcast.92, bf16[1,32,6,128,128]{4,3,2,1,0:T(8,128)(2,1)} %param.10), kind=kOutput, calls=%fused_computation.19 | convolution fusion | flops 19327352832 | bytes 65011712 | tf_op jit(solution)/shard_map/arjc,rjoc->aro/dot_general | solution.py:34
  111.7 6.4 all-to-all-start
  118.1 9.0 copy.31
  127.1 175.0 %all-to-all-done = f32[512,32,128]{2,0,1:T(8,128)} async-done(((f32[512,32,128]{2,0,1:T(8,128)}), f32[512,32,128]{2,0,1:T(8,128)}, u32[]{:S(2)}, u32[]{:S(2)}) %all-to-all-start) | async-done | bytes 8388640 | tf_op jit(solution)/shard_map/all_to_all | solution.py:37
  307.1 7.7 copy.28
  314.7 22.2 %gather_fusion.1 = f32[192,128,4,128]{3,1,2,0:T(8,128)} fusion(f32[32,128,4,128]{3,1,0,2:T(8,128)} %bitcast.91, s32[1024]{0:T(1024)S(1)} %pad_clamp_fusion), kind=kCustom, calls=%fused_computation.1.clone | custom fusion | bytes 100664064 | tf_op jit(solution)/shard_map/jit(_take)/gather | solution.py:40
  337.0 34.9 %broadcast_select_fusion.1 = f32[192,128,4,128]{3,1,2,0:T(8,128)} fusion(f32[192,128,4,128]{3,1,2,0:T(8,128)} %gather_fusion.1, pred[192]{0:T(512)(128)(4,1)S(1)} %compare_and_fusion), kind=kLoop, calls=%fused_computation.5 | loop fusion | flops 12582912 | bytes 100663488 | tf_op jit(solution)/shard_map/jit(_take)/select_n | solution.py:40
  371.9 48.2 %fusion.14 = f32[4,128,32,128]{3,1,0,2:T(8,128)} fusion(f32[32,6,128,4,128]{4,2,3,1,0:T(8,128)} %bitcast.95, bf16[1,32,6,128,128]{4,3,2,1,0:T(8,128)(2,1)} %param.10), kind=kOutput, calls=%fused_computation.21 | convolution fusion | flops 19327352832 | bytes 65011712 | tf_op jit(solution)/shard_map/rjoc,rjcnm->nmro/dot_general | solution.py:44
  420.1 8.2 copy.30
  428.4 11.7 copy.55
  440.1 50.7 %all-to-all-done.1 = f32[512,32,128]{0,2,1:T(8,128)} async-done(((f32[512,32,128]{0,2,1:T(8,128)}), f32[512,32,128]{0,2,1:T(8,128)}, u32[]{:S(2)}, u32[]{:S(2)}) %all-to-all-start.1) | async-done | bytes 8388640 | tf_op jit(solution)/shard_map/all_to_all | solution.py:18
  490.9 8.4 copy.33
  499.2 11.7 copy.50
  511.0 102.6 %all-reduce.3.cloned.1.call-done = f32[512,4096]{1,0:T(8,128)} async-done(((f32[512,4096]{1,0:T(8,128)}), f32[512,4096]{1,0:T(8,128)}) %all-reduce.3.cloned.1.call-update) | async-done | bytes 8388624 | tf_op jit(solution)/shard_map/psum | solution.py:49
  613.6 11.3 bitcast_subtract_fusion
  624.9 9.0 copy.34
  633.9 8.9 copy.35
  642.8 22.2 %gather_fusion.2 = f32[192,512,128]{2,1,0:T(8,128)} fusion(f32[512,32,128]{2,0,1:T(8,128)} %copy.35, s32[1024]{0:T(1024)S(1)} %pad_clamp_fusion), kind=kCustom, calls=%fused_computation.2.clone | custom fusion | bytes 100664064 | tf_op jit(solution)/shard_map/jit(_take)/gather | solution.py:30
  665.0 34.0 %broadcast_select_fusion.2 = f32[192,512,128]{2,1,0:T(8,128)} fusion(f32[192,512,128]{2,1,0:T(8,128)} %gather_fusion.2, pred[192]{0:T(512)(128)(4,1)S(1)} %compare_and_fusion), kind=kLoop, calls=%fused_computation.6 | loop fusion | flops 12582912 | bytes 100663488 | tf_op jit(solution)/shard_map/jit(_take)/select_n | solution.py:30
  699.1 30.1 %fusion.11 = f32[512,32,128]{2,0,1:T(8,128)} fusion(f32[512,32,6,128]{3,0,2,1:T(8,128)} %bitcast.93, bf16[1,32,6,128,128]{4,3,2,1,0:T(8,128)(2,1)} %param.10), kind=kOutput, calls=%fused_computation.20 | convolution fusion | flops 19327352832 | bytes 65011712 | tf_op jit(solution)/shard_map/arjc,rjoc->aro/dot_general | solution.py:34
  729.2 188.9 %all_to_all.45 = f32[512,32,128]{2,0,1:T(8,128)S(1)} all-to-all(f32[512,32,128]{2,0,1:T(8,128)} %fusion.11), channel_id=1, replica_groups=mesh['op'=4,'str'=8] {'str'}, dimensions={1} | all-to-all | bytes 16777216 | tf_op jit(solution)/shard_map/all_to_all | solution.py:37
  922.1 22.2 %gather_fusion.3 = f32[192,128,4,128]{3,1,2,0:T(8,128)} fusion(f32[32,128,4,128]{3,1,0,2:T(8,128)} %bitcast.90, s32[1024]{0:T(1024)S(1)} %pad_clamp_fusion), kind=kCustom, calls=%fused_computation.3.clone | custom fusion | bytes 100664064 | tf_op jit(solution)/shard_map/jit(_take)/gather | solution.py:40
  944.3 34.9 %broadcast_select_fusion = f32[192,128,4,128]{3,1,2,0:T(8,128)} fusion(f32[192,128,4,128]{3,1,2,0:T(8,128)} %gather_fusion.3, pred[192]{0:T(512)(128)(4,1)S(1)} %compare_and_fusion), kind=kLoop, calls=%fused_computation.4 | loop fusion | flops 12582912 | bytes 100663488 | tf_op jit(solution)/shard_map/jit(_take)/select_n | solution.py:40
  979.3 47.8 %fusion.17 = f32[4,128,32,128]{3,1,0,2:T(8,128)} fusion(f32[32,6,128,4,128]{4,2,3,1,0:T(8,128)} %bitcast.94, bf16[1,32,6,128,128]{4,3,2,1,0:T(8,128)(2,1)} %param.10), kind=kOutput, calls=%fused_computation.22 | convolution fusion | flops 19327352832 | bytes 65011712 | tf_op jit(solution)/shard_map/rjoc,rjcnm->nmro/dot_general | solution.py:44
  1027.1 8.2 copy.38
  1035.4 11.8 copy.54
  1047.1 170.5 %all-reduce.5.cloned.1.call-done = f32[512,4096]{1,0:T(8,128)} async-done(((f32[512,4096]{1,0:T(8,128)}), f32[512,4096]{1,0:T(8,128)}) %all-reduce.5.cloned.1.call-update) | async-done | bytes 8388624 | tf_op jit(solution)/shard_map/psum | solution.py:49
  1217.6 11.3 sub.7
  (11 shorter events, 9.9 us)
Async XLA Ops:
  111.7 190.3 %all-to-all-start = ((f32[512,32,128]{2,0,1:T(8,128)}), f32[512,32,128]{2,0,1:T(8,128)}, u32[]{:S(2)}, u32[]{:S(2)}) async-start(f32[512,32,128]{2,0,1:T(8,128)} %fusion.8), calls=%async_computation | async-start | bytes 16777216 | tf_op jit(solution)/shard_map/all_to_all | solution.py:37
  302.1 188.8 %all-to-all-start.1 = ((f32[512,32,128]{0,2,1:T(8,128)}), f32[512,32,128]{0,2,1:T(8,128)}, u32[]{:S(2)}, u32[]{:S(2)}) async-start(f32[512,32,128]{0,2,1:T(8,128)} %bitcast.97), calls=%async_computation.1 | async-start | bytes 16777216 | tf_op jit(solution)/shard_map/all_to_all | solution.py:18
  307.0 306.5 %all-reduce.3.cloned.1.call-start = ((), (), s32[]{:S(2)}) async-start(), calls=%async_computation.3 | async-start | bytes 16777216 | tf_op jit(solution)/shard_map/psum | solution.py:49
  440.1 777.5 %all-reduce.5.cloned.1.call-start = ((), (), s32[]{:S(2)}) async-start(), calls=%async_computation.4 | async-start | bytes 16777216 | tf_op jit(solution)/shard_map/psum | solution.py:49
Sparse Core Ops, SparseCore 0:
  440.2 173.3 all-reduce.2
  1047.3 170.2 all-reduce.4
where the time goes:
time: 1250 us; the launch traced here: 1240 us
  waiting for transfers between devices  499 us (40%)
  local copies, waits for them, and re-layouts  206 us (16%)
  blocking collectives  189 us (15%)
  other arithmetic  161 us (13%)
  matrix products  156 us (12%)
  between operations  13.9 us (1%)
    psum x2, waiting for transfers between devices, per_device(): updated = step_scale * lax.psum(summed, 'op') - earlier  273 us
    all_to_all x1, blocking collectives, per_device(): lax.all_to_all(beta_side, 'str', split_axis=1, concat_axis=0, tiled=True)  189 us
    all_to_all x1, waiting for transfers between devices, per_device(): lax.all_to_all(beta_side, 'str', split_axis=1, concat_axis=0, tiled=True)  175 us
    dot_general x2, matrix products, per_device(): jnp.einsum('rjoc,rjcnm->nmro', term_factors, grouped, precision=lax.Preci...  96.1 us
    select_n x3, other arithmetic, per_device(): jnp.take(received.reshape(block_count, block_size, group_count, item_coun...  69.9 us
    select_n x2, other arithmetic, per_device(): jnp.take(current.reshape(row_count, block_count, block_size), column_list...  68.1 us
    dot_general x2, matrix products, per_device(): jnp.einsum('arjc,rjoc->aro', gathered, term_factors, precision=lax.Precis...  60.2 us
    unnamed x6, local copies, waits for them, and re-layouts  53.9 us
  transfers between devices with their start and end apart: 4, of which 4 were waited for; matrix products, arithmetic and copies ran while one was open for 13% of the time, Pallas kernels for 0%

commit v1 on v0

--- a/solution.py
+++ b/solution.py
@@ -5,6 +5,29 @@
 from jax.sharding import PartitionSpec as P
 
 STEPS = 2
+
+
+def split_up(x, dim, size):
+    shape = x.shape
+    pieces = x.reshape(*shape[:dim], size, shape[dim] // size, *shape[dim + 1 :])
+    return jnp.moveaxis(pieces, dim, 0)
+
+
+def in_order(parts, dim):
+    parts = jnp.moveaxis(parts, 0, dim)
+    shape = parts.shape
+    return parts.reshape(*shape[:dim], shape[dim] * shape[dim + 1], *shape[dim + 2 :])
+
+
+def exchange_directly(shard, axis, split_dim, concat_dim):
+    length, index = (lax.axis_size(axis), lax.axis_index(axis))
+    blocks = split_up(shard, split_dim, length)
+    gathered = [blocks[index]]
+    for hop in range(1, length):
+        sent = blocks[(index + hop) % length]
+        gathered.append(lax.ppermute(sent, axis, [(i, (i + hop) % length) for i in range(length)]))
+    blocks = jnp.stack(gathered)[(index - jnp.arange(length)) % length]
+    return in_order(blocks, concat_dim)
 
 
 def per_device(coeffs, previous, block_values, block_cols):
@@ -15,13 +38,7 @@
     block_size = block_values.shape[-1]
     block_count = full_width // block_size
     slot_count = block_cols.shape[2]
-    regrouped = lax.all_to_all(
-        previous.reshape(row_count, block_count, block_size),
-        "str",
-        split_axis=1,
-        concat_axis=0,
-        tiled=True,
-    )
+    regrouped = exchange_directly(previous.reshape(row_count, block_count, block_size), "str", 1, 0)
     earlier = regrouped.reshape(full_width, row_count).T
     current = coeffs
     for step_index in range(STEPS):

time: 1250 us -> 1300 us (1.040)
  blocking collectives: 189 us -> 425 us
  waiting for transfers between devices: 499 us -> 273 us
  local copies, waits for them, and re-layouts: 206 us -> 231 us
  starting transfers between devices: 11.4 us -> 25.1 us
    all_to_all x1 -> x2, blocking collectives: 189 us -> 425 us  [per_device(): lax.all_to_all(beta_side, 'str', split_axis=1, concat_axis=0, tiled=True)]
    all_to_all x2 -> x0, waiting for transfers between devices: 226 us -> none  [the longest x1 175 us: per_device(): lax.all_to_all(beta_side, 'str', split_axis=1, concat_axis=0, tiled=True)]
    psum x2, waiting for transfers between devices: 273 us -> 171 us  [per_device(): updated = step_scale * lax.psum(summed, 'op') - earlier]
    ppermute x0 -> x7, waiting for transfers between devices: none -> 102 us  [exchange_directly(): lax.ppermute(sent, axis, [(i, (i + hop) % length) for i in range(length)])]
    ppermute x0 -> x7, starting transfers between devices: none -> 25 us  [exchange_directly(): lax.ppermute(sent, axis, [(i, (i + hop) % length) for i in range(length)])]
    gather x0 -> x2, local copies, waits for them, and re-layouts: none -> 18.3 us  [exchange_directly(): blocks = jnp.stack(gathered)[(index - jnp.arange(length)) % length]]
    another operation x0 -> x3, local copies, waits for them, and re-layouts: none -> 16.5 us  [the longest x1 10.9 us: split_up(): pieces = x.reshape(*shape[:dim], size, shape[dim] // size, *shape[dim + 1:])]
    unnamed x6 -> x19, local copies, waits for them, and re-layouts: 53.9 us -> 55.8 us
  transfers between devices with their start and end apart: 4 -> 9, of which waited for: 4 -> 5; matrix products, arithmetic and copies ran while one was open for 13% -> 4% of each run, Pallas kernels for 0% -> 0%
where the time goes in v1:
time: 1300 us; the launch traced here: 1290 us
  blocking collectives  425 us (33%)
  waiting for transfers between devices  273 us (21%)
  local copies, waits for them, and re-layouts  231 us (18%)
  other arithmetic  161 us (12%)
  matrix products  157 us (12%)
  starting transfers between devices  25.1 us (2%)
  between operations  14.1 us (1%)
    all_to_all x2, blocking collectives, per_device(): lax.all_to_all(beta_side, 'str', split_axis=1, concat_axis=0, tiled=True)  425 us
    psum x2, waiting for transfers between devices, per_device(): updated = step_scale * lax.psum(summed, 'op') - earlier  171 us
    ppermute x7, waiting for transfers between devices, exchange_directly(): lax.ppermute(sent, axis, [(i, (i + hop) % length) for i in range(length)])  102 us
    dot_general x2, matrix products, per_device(): jnp.einsum('rjoc,rjcnm->nmro', term_factors, grouped, precision=lax.Preci...  96.3 us
    select_n x3, other arithmetic, per_device(): jnp.take(received.reshape(block_count, block_size, group_count, item_coun...  69.9 us
    select_n x2, other arithmetic, per_device(): jnp.take(current.reshape(row_count, block_count, block_size), column_list...  68.1 us
    dot_general x2, matrix products, per_device(): jnp.einsum('arjc,rjoc->aro', gathered, term_factors, precision=lax.Precis...  60.2 us
    unnamed x19, local copies, waits for them, and re-layouts  55.8 us
  transfers between devices with their start and end apart: 9, of which 5 were waited for; matrix products, arithmetic and copies ran while one was open for 4% of the time, Pallas kernels for 0%

profile of v1, /device:TPU:0, one launch (start us, length us, event | category | flops | bytes accessed | tf_op | source)
XLA Modules:
  0.0 1286.1 jit_solution(16999478889715099370)
XLA Ops:
  7.4 9.0 copy.33
  16.4 8.9 copy.34
  25.3 22.2 %gather_fusion.1 = f32[192,512,128]{2,1,0:T(8,128)} fusion(f32[512,32,128]{2,0,1:T(8,128)} %copy.34, s32[1024]{0:T(1024)S(1)} %pad_clamp_fusion.1), kind=kCustom, calls=%fused_computation.clone | custom fusion | bytes 100664064 | tf_op jit(solution)/shard_map/jit(_take)/gather | solution.py:47
  47.6 34.1 %broadcast_select_fusion.3 = f32[192,512,128]{2,1,0:T(8,128)} fusion(f32[192,512,128]{2,1,0:T(8,128)} %gather_fusion.1, pred[192]{0:T(512)(128)(4,1)S(1)} %compare_and_fusion), kind=kLoop, calls=%fused_computation.8 | loop fusion | flops 12582912 | bytes 100663488 | tf_op jit(solution)/shard_map/jit(_take)/select_n | solution.py:47
  81.6 30.1 %fusion.8 = f32[512,32,128]{2,0,1:T(8,128)} fusion(f32[512,32,6,128]{3,0,2,1:T(8,128)} %bitcast.129, bf16[1,32,6,128,128]{4,3,2,1,0:T(8,128)(2,1)} %param.10), kind=kOutput, calls=%fused_computation.20 | convolution fusion | flops 19327352832 | bytes 65011712 | tf_op jit(solution)/shard_map/arjc,rjoc->aro/dot_general | solution.py:51
  111.7 190.2 %all_to_all.30 = f32[512,32,128]{2,0,1:T(8,128)S(1)} all-to-all(f32[512,32,128]{2,0,1:T(8,128)} %fusion.8), channel_id=1, replica_groups=mesh['op'=4,'str'=8] {'str'}, dimensions={1} | all-to-all | bytes 16777216 | tf_op jit(solution)/shard_map/all_to_all | solution.py:54
  305.9 22.2 %gather_fusion.2 = f32[192,128,4,128]{3,1,2,0:T(8,128)} fusion(f32[32,128,4,128]{3,1,0,2:T(8,128)} %bitcast.128, s32[1024]{0:T(1024)S(1)} %pad_clamp_fusion.1), kind=kCustom, calls=%fused_computation.1.clone | custom fusion | bytes 100664064 | tf_op jit(solution)/shard_map/jit(_take)/gather | solution.py:57
  328.2 34.9 %broadcast_select_fusion.1 = f32[192,128,4,128]{3,1,2,0:T(8,128)} fusion(f32[192,128,4,128]{3,1,2,0:T(8,128)} %gather_fusion.2, pred[192]{0:T(512)(128)(4,1)S(1)} %compare_and_fusion), kind=kLoop, calls=%fused_computation.6 | loop fusion | flops 12582912 | bytes 100663488 | tf_op jit(solution)/shard_map/jit(_take)/select_n | solution.py:57
  363.1 48.3 %fusion.14 = f32[4,128,32,128]{3,1,0,2:T(8,128)} fusion(f32[32,6,128,4,128]{4,2,3,1,0:T(8,128)} %bitcast.132, bf16[1,32,6,128,128]{4,3,2,1,0:T(8,128)(2,1)} %param.10), kind=kOutput, calls=%fused_computation.22 | convolution fusion | flops 19327352832 | bytes 65011712 | tf_op jit(solution)/shard_map/rjoc,rjcnm->nmro/dot_general | solution.py:61
  411.4 8.2 copy.37
  419.7 11.7 copy.85
  431.5 10.9 reshape_reshape.13
  453.0 20.8 %collective-permute-done = f32[512,4,128]{2,0,1:T(8,128)S(1)} collective-permute-done((f32[512,4,128]{2,0,1:T(8,128)S(1)}, f32[512,4,128]{2,0,1:T(8,128)S(1)}, u32[]{:S(2)}, u32[]{:S(2)}) %collective-permute-start) | collective-permute-done | bytes 1048608 | tf_op jit(solution)/shard_map/ppermute | solution.py:28
  475.2 20.6 %collective-permute-start.6 = (f32[512,4,128]{2,0,1:T(8,128)S(1)}, f32[512,4,128]{2,0,1:T(8,128)S(1)}, u32[]{:S(2)}, u32[]{:S(2)}) collective-permute-start(f32[512,4,128]{2,0,1:T(8,128)S(1)} %bitcast.143), channel_id=1, source_target_pairs={{0,7},{1,0},{2,1},{3,2},{4,3},{5,4},{6,5},{7,6},{8,15},{9,8},{10,9... | collective-permute-start | bytes 3145736 | tf_op jit(solution)/shard_map/ppermute | solution.py:28
  496.8 67.3 %collective-permute-done.2 = f32[512,4,128]{2,0,1:T(8,128)S(1)} collective-permute-done((f32[512,4,128]{2,0,1:T(8,128)S(1)}, f32[512,4,128]{2,0,1:T(8,128)S(1)}, u32[]{:S(2)}, u32[]{:S(2)}) %collective-permute-start.2) | collective-permute-done | bytes 1048608 | tf_op jit(solution)/shard_map/ppermute | solution.py:28
  568.4 13.9 %collective-permute-done.6 = f32[512,4,128]{2,0,1:T(8,128)S(1)} collective-permute-done((f32[512,4,128]{2,0,1:T(8,128)S(1)}, f32[512,4,128]{2,0,1:T(8,128)S(1)}, u32[]{:S(2)}, u32[]{:S(2)}) %collective-permute-start.6) | collective-permute-done | bytes 1048608 | tf_op jit(solution)/shard_map/ppermute | solution.py:28
  591.4 10.3 copy.46
  601.7 14.7 %copy.70 = f32[64,8,8,512]{3,1,2,0:T(8,128)} copy(f32[64,8,8,512]{3,2,1,0:T(8,128)} %bitcast.138) | data formatting | bytes 16777216
  616.4 11.3 bitcast_subtract_fusion
  627.7 9.0 copy.47
  636.7 8.9 copy.48
  645.7 22.7 %gather_fusion.3 = f32[192,512,128]{2,1,0:T(8,128)} fusion(f32[512,32,128]{2,0,1:T(8,128)} %copy.48, s32[1024]{0:T(1024)S(1)} %pad_clamp_fusion.1), kind=kCustom, calls=%fused_computation.2.clone | custom fusion | bytes 100664064 | tf_op jit(solution)/shard_map/jit(_take)/gather | solution.py:47
  668.3 34.1 %broadcast_select_fusion.2 = f32[192,512,128]{2,1,0:T(8,128)} fusion(f32[192,512,128]{2,1,0:T(8,128)} %gather_fusion.3, pred[192]{0:T(512)(128)(4,1)S(1)} %compare_and_fusion), kind=kLoop, calls=%fused_computation.7 | loop fusion | flops 12582912 | bytes 100663488 | tf_op jit(solution)/shard_map/jit(_take)/select_n | solution.py:47
  702.4 30.1 %fusion.11 = f32[512,32,128]{2,0,1:T(8,128)} fusion(f32[512,32,6,128]{3,0,2,1:T(8,128)} %bitcast.130, bf16[1,32,6,128,128]{4,3,2,1,0:T(8,128)(2,1)} %param.10), kind=kOutput, calls=%fused_computation.21 | convolution fusion | flops 19327352832 | bytes 65011712 | tf_op jit(solution)/shard_map/arjc,rjoc->aro/dot_general | solution.py:51
  732.5 235.1 %all_to_all.31 = f32[512,32,128]{2,0,1:T(8,128)S(1)} all-to-all(f32[512,32,128]{2,0,1:T(8,128)} %fusion.11), channel_id=1, replica_groups=mesh['op'=4,'str'=8] {'str'}, dimensions={1} | all-to-all | bytes 16777216 | tf_op jit(solution)/shard_map/all_to_all | solution.py:54
  971.6 22.2 %gather_fusion.4 = f32[192,128,4,128]{3,1,2,0:T(8,128)} fusion(f32[32,128,4,128]{3,1,0,2:T(8,128)} %bitcast.127, s32[1024]{0:T(1024)S(1)} %pad_clamp_fusion.1), kind=kCustom, calls=%fused_computation.3.clone | custom fusion | bytes 100664064 | tf_op jit(solution)/shard_map/jit(_take)/gather | solution.py:57
  993.8 34.9 %broadcast_select_fusion = f32[192,128,4,128]{3,1,2,0:T(8,128)} fusion(f32[192,128,4,128]{3,1,2,0:T(8,128)} %gather_fusion.4, pred[192]{0:T(512)(128)(4,1)S(1)} %compare_and_fusion), kind=kLoop, calls=%fused_computation.5 | loop fusion | flops 12582912 | bytes 100663488 | tf_op jit(solution)/shard_map/jit(_take)/select_n | solution.py:57
  1028.8 48.0 %fusion.17 = f32[4,128,32,128]{3,1,0,2:T(8,128)} fusion(f32[32,6,128,4,128]{4,2,3,1,0:T(8,128)} %bitcast.131, bf16[1,32,6,128,128]{4,3,2,1,0:T(8,128)(2,1)} %param.10), kind=kOutput, calls=%fused_computation.23 | convolution fusion | flops 19327352832 | bytes 65011712 | tf_op jit(solution)/shard_map/rjoc,rjcnm->nmro/dot_general | solution.py:61
  1076.8 8.2 copy.51
  1085.0 11.8 copy.84
  1096.8 170.7 %all-reduce.5.cloned.1.call-done = f32[512,4096]{1,0:T(8,128)} async-done(((f32[512,4096]{1,0:T(8,128)}), f32[512,4096]{1,0:T(8,128)}) %all-reduce.5.cloned.1.call-update) | async-done | bytes 8388624 | tf_op jit(solution)/shard_map/psum | solution.py:66
  1267.5 11.3 sub.22
  (41 shorter events, 35.2 us)
Async XLA Ops:
  6.5 609.9 %all-reduce.3.cloned.1.call-start = ((), (), s32[]{:S(2)}) async-start(), calls=%async_computation.2 | async-start | bytes 16777216 | tf_op jit(solution)/shard_map/psum | solution.py:66
  431.4 836.1 %all-reduce.5.cloned.1.call-start = ((), (), s32[]{:S(2)}) async-start(), calls=%async_computation.3 | async-start | bytes 16777216 | tf_op jit(solution)/shard_map/psum | solution.py:66
  447.0 26.8 %collective-permute-start = (f32[512,4,128]{2,0,1:T(8,128)S(1)}, f32[512,4,128]{2,0,1:T(8,128)S(1)}, u32[]{:S(2)}, u32[]{:S(2)}) collective-permute-start(f32[512,4,128]{2,0,1:T(8,128)S(1)} %bitcast.149), channel_id=1, source_target_pairs={{0,1},{1,2},{2,3},{3,4},{4,5},{5,6},{6,7},{7,0},{8,9},{9,10},{10,1... | collective-permute-start | bytes 3145736 | tf_op jit(solution)/shard_map/ppermute | solution.py:28
  447.1 28.1 %collective-permute-start.1 = (f32[512,4,128]{2,0,1:T(8,128)S(1)}, f32[512,4,128]{2,0,1:T(8,128)S(1)}, u32[]{:S(2)}, u32[]{:S(2)}) collective-permute-start(f32[512,4,128]{2,0,1:T(8,128)S(1)} %bitcast.148), channel_id=1, source_target_pairs={{0,2},{1,3},{2,4},{3,5},{4,6},{5,7},{6,0},{7,1},{8,10},{9,11},{10,... | collective-permute-start | bytes 3145736 | tf_op jit(solution)/shard_map/ppermute | solution.py:28
  447.3 116.8 %collective-permute-start.2 = (f32[512,4,128]{2,0,1:T(8,128)S(1)}, f32[512,4,128]{2,0,1:T(8,128)S(1)}, u32[]{:S(2)}, u32[]{:S(2)}) collective-permute-start(f32[512,4,128]{2,0,1:T(8,128)S(1)} %bitcast.147), channel_id=1, source_target_pairs={{0,3},{1,4},{2,5},{3,6},{4,7},{5,0},{6,1},{7,2},{8,11},{9,12},{10,... | collective-permute-start | bytes 3145736 | tf_op jit(solution)/shard_map/ppermute | solution.py:28
  449.1 116.1 %collective-permute-start.3 = (f32[512,4,128]{2,0,1:T(8,128)S(1)}, f32[512,4,128]{2,0,1:T(8,128)S(1)}, u32[]{:S(2)}, u32[]{:S(2)}) collective-permute-start(f32[512,4,128]{2,0,1:T(8,128)S(1)} %bitcast.146), channel_id=1, source_target_pairs={{0,4},{1,5},{2,6},{3,7},{4,0},{5,1},{6,2},{7,3},{8,12},{9,13},{10,... | collective-permute-start | bytes 3145736 | tf_op jit(solution)/shard_map/ppermute | solution.py:28
  451.6 114.6 %collective-permute-start.4 = (f32[512,4,128]{2,0,1:T(8,128)S(1)}, f32[512,4,128]{2,0,1:T(8,128)S(1)}, u32[]{:S(2)}, u32[]{:S(2)}) collective-permute-start(f32[512,4,128]{2,0,1:T(8,128)S(1)} %bitcast.145), channel_id=1, source_target_pairs={{0,5},{1,6},{2,7},{3,0},{4,1},{5,2},{6,3},{7,4},{8,13},{9,14},{10,... | collective-permute-start | bytes 3145736 | tf_op jit(solution)/shard_map/ppermute | solution.py:28
  473.8 93.5 %collective-permute-start.5 = (f32[512,4,128]{2,0,1:T(8,128)S(1)}, f32[512,4,128]{2,0,1:T(8,128)S(1)}, u32[]{:S(2)}, u32[]{:S(2)}) collective-permute-start(f32[512,4,128]{2,0,1:T(8,128)S(1)} %bitcast.144), channel_id=1, source_target_pairs={{0,6},{1,7},{2,0},{3,1},{4,2},{5,3},{6,4},{7,5},{8,14},{9,15},{10,... | collective-permute-start | bytes 3145736 | tf_op jit(solution)/shard_map/ppermute | solution.py:28
  475.2 107.1 %collective-permute-start.6 = (f32[512,4,128]{2,0,1:T(8,128)S(1)}, f32[512,4,128]{2,0,1:T(8,128)S(1)}, u32[]{:S(2)}, u32[]{:S(2)}) collective-permute-start(f32[512,4,128]{2,0,1:T(8,128)S(1)} %bitcast.143), channel_id=1, source_target_pairs={{0,7},{1,0},{2,1},{3,2},{4,3},{5,4},{6,5},{7,6},{8,15},{9,8},{10,9... | collective-permute-start | bytes 3145736 | tf_op jit(solution)/shard_map/ppermute | solution.py:28
Sparse Core Ops, SparseCore 0:
  431.5 170.8 all-reduce.2
  1096.9 170.5 all-reduce.4
